TPU v7x, 512 devices: a whole 4x4x16 slice. The times are simulated.
512 devices in a mesh: dp: 4 (over y), expert: 128 (over z, x, core).
Axes of the slice: x: 4, y: 4, z: 16, core: 2. Of those that a mesh axis runs over, the one named last changes fastest.
Arguments:
- grad_out: bfloat16 [16384, 4096], P(('dp', 'expert')), may hold values from -6 to 6
- expert_ids: int32 [16384, 8], P(('dp', 'expert')), may hold values from 0 to 127, all different within a row; in each aligned block of 32 rows (0 to 31, 32 to 63, ...) at most 2 rows name the same one
- route_weights: float32 [16384, 8], P(('dp', 'expert')), may hold values from 0.02 to 0.2
- hidden_act: bfloat16 [4, 128, 256, 1536], P('dp', 'expert'), may hold values from -6 to 6
- projection: bfloat16 [128, 1536, 256], P('expert', 'dp'), may hold values from -0.15625 to 0.15625
Outputs:
- projected_grad: bfloat16 [128, 4096, 256], P('expert', 'dp')
Inputs may be any that keep to these rules, and one draw needn't show every extreme that they name: `expert_ids`: each row names 8 different experts. Among the 32 tokens of one device (aligned blocks of rows), no expert is named more than 2 times, a bound that some block reaches.
All inputs are finite; a program needn't handle non-finite values.
Results may differ from a plain program's by a relative error of at most 0.0058.
Values may be sent and summed in bfloat16 or wider, within the bound.
No kernel may reach another device: no remote copies, remote signals or barrier semaphores. Data moves between devices by JAX's collectives and lax.ppermute only.
A program may use at most 64 MiB of HBM per device.

v0:
```python
import jax
import jax.numpy as jnp
from jax import lax
from jax.sharding import PartitionSpec as P


def shards(grad_out, expert_ids, route_weights, hidden_act, projection):
    token_count = grad_out.shape[0]
    width = grad_out.shape[1]
    top_count = expert_ids.shape[1]
    expert_count = lax.axis_size("expert")
    slot_count = hidden_act.shape[2]
    capacity = slot_count // expert_count
    route_total = token_count * top_count
    routed = expert_ids.reshape(-1)
    onehot = (routed[:, None] == jnp.arange(expert_count, dtype=jnp.int32)[None, :]).astype(
        jnp.int32
    )
    earlier = jnp.cumsum(onehot, axis=0) - onehot
    position = jnp.sum(earlier * onehot, axis=1)
    slot = routed * capacity + position
    table = jnp.full((expert_count * capacity,), -1, jnp.int32)
    table = table.at[slot].set(jnp.arange(route_total, dtype=jnp.int32))
    valid = table >= 0
    picked = jnp.maximum(table, 0)
    rows = grad_out[picked // top_count].astype(jnp.float32)
    weight = route_weights.reshape(-1)[picked]
    weighted = jnp.where(valid[:, None], weight[:, None] * rows, 0.0).astype(jnp.bfloat16)
    outgoing = weighted.reshape(expert_count, capacity, width)
    hidden = hidden_act[0, 0]
    reduced = jnp.dot(
        hidden,
        lax.all_gather(projection[0], "dp", axis=0, tiled=True),
        preferred_element_type=jnp.float32,
    ).astype(jnp.bfloat16)
    arrived = lax.all_to_all(outgoing, "expert", split_axis=0, concat_axis=0, tiled=True).reshape(
        slot_count, width
    )
    share = lax.psum_scatter(
        lax.dot_general(
            arrived, reduced, (((0,), (0,)), ((), ())), preferred_element_type=jnp.float32
        ),
        "dp",
        scatter_dimension=0,
        tiled=True,
    )
    return share.astype(jnp.bfloat16)[None]


def solution(mesh):
    in_specs = (
        P(("dp", "expert"), None),
        P(("dp", "expert"), None),
        P(("dp", "expert"), None),
        P("dp", "expert", None, None),
        P("expert", "dp", None),
    )
    out_specs = P("expert", "dp", None)
    return jax.shard_map(shards, mesh=mesh, in_specs=in_specs, out_specs=out_specs, check_vma=False)
```

profile of v0, /device:TPU:1, one launch (start us, length us, event | category | flops | bytes accessed | tf_op | source)
XLA Modules:
  0.0 209.0 jit_solution(662351124627535418)
XLA Ops:
  6.5 0.0 copy-start
  6.5 0.0 copy-start.1
  6.5 0.8 copy.7
  7.4 0.1 eq.29
  7.5 0.1 eq.25
  7.6 0.7 broadcast_multiply_fusion
  8.3 0.1 copy.9
  8.4 0.2 fusion.5
  8.7 0.1 copy.6
  8.8 0.1 mul.32
  8.8 0.2 fusion.7
  9.1 1.4 scatter_custom_fusion
  10.5 0.0 copy-done.1
  10.5 1.8 gather_fusion.1
  12.4 0.0 copy-start.3
  12.4 4.0 %reshape.71 = f32[128,2,4096]{2,1,0:T(2,128)} reshape(bf16[256,4096]{1,0:T(8,128)(2,1)S(1)} %gather_fusion.1) | data formatting | bytes 6291456 | tf_op jit(solution)/shard_map/convert_element_type | solution.py:26
  16.4 0.0 copy-done.3
  16.4 0.1 copy.11
  16.4 0.1 reshape.69
  16.5 1.9 gather_fusion
  18.5 0.1 mul.34
  18.6 0.2 broadcast_in_dim.31
  18.8 6.9 %select_convert_fusion = bf16[128,2,4096]{2,1,0:T(2,128)(2,1)} fusion(f32[128,2,4096]{2,1,0:T(2,128)} %reshape.71, pred[128,2]{1,0:T(8,128)(4,1)S(1)} %broadcast_in_dim.31, f32[128,2]{1,0:T(8,128)S(1)} %mul.34), kind=kLoop, calls=%fused_computation.3 | loop fusion | flops 3145728 | bytes 6292736 | tf_op jit(solution)/shard_map/convert_element_type | solution.py:28
  25.7 0.0 copy-start.2
  25.7 20.5 %all-to-all-start = ((bf16[128,2,4096]{2,1,0:T(2,128)(2,1)}), bf16[128,2,4096]{2,1,0:T(2,128)(2,1)S(1)}, u32[]{:S(2)}, u32[]{:S(2)}) async-start(bf16[128,2,4096]{2,1,0:T(2,128)(2,1)} %select_convert_fusion), calls=%async_computation | async-start | bytes 4194304 | tf_op jit(solution)/shard_map/all_to_all | solution.py:36
  46.3 0.0 reduce-scatter.2.cloned.1.call-start
  46.3 0.0 copy-done.2
  46.3 13.2 %all-gather = bf16[1,1536,256]{2,1,0:T(8,128)(2,1)} all-gather(bf16[1,384,256]{2,1,0:T(8,128)(2,1)S(1)} %copy-done.2), channel_id=2, replica_groups=mesh['dp'=4,'expert'=128] {'dp'}, dimensions={1}, use_global_device_ids=true | all-gather | bytes 983040 | tf_op jit(solution)/shard_map/all_gather | solution.py:33
  59.5 82.7 %all-to-all-done = bf16[128,2,4096]{2,1,0:T(2,128)(2,1)S(1)} async-done(((bf16[128,2,4096]{2,1,0:T(2,128)(2,1)}), bf16[128,2,4096]{2,1,0:T(2,128)(2,1)S(1)}, u32[]{:S(2)}, u32[]{:S(2)}) %all-to-all-start) | async-done | bytes 2097184 | tf_op jit(solution)/shard_map/all_to_all | solution.py:36
  142.2 2.2 %reshape.70 = bf16[256,4096]{1,0:T(8,128)(2,1)} reshape(bf16[128,2,4096]{2,1,0:T(2,128)(2,1)S(1)} %all-to-all-done) | data formatting | bytes 4194304 | tf_op jit(solution)/shard_map/reshape | solution.py:36
  144.4 0.0 copy-done
  144.4 5.1 %fusion = f32[4096,256]{1,0:T(8,128)} fusion(bf16[256,4096]{1,0:T(8,128)(2,1)} %reshape.70, bf16[1,1536,256]{2,1,0:T(8,128)(2,1)} %all-gather, bf16[1,1,256,1536]{3,2,1,0:T(8,128)(2,1)S(1)} %copy-done), kind=kOutput, calls=%fused_computation.5 | convolution fusion | flops 738263040 | bytes 7864320 | tf_op jit(solution)/shard_map/dot_general | solution.py:40
  149.5 0.0 reduce-scatter.2.cloned.1.call-update
  149.5 50.6 %reduce-scatter.2.cloned.1.call-done = f32[1024,256]{1,0:T(8,128)} async-done(((f32[4096,256]{1,0:T(8,128)}), f32[1024,256]{1,0:T(8,128)}) %reduce-scatter.2.cloned.1.call-update) | async-done | bytes 1048592 | tf_op jit(solution)/shard_map/reduce_scatter | solution.py:39
  200.1 2.1 convert_bitcast_fusion
  (11 shorter events, 0.1 us)
Async XLA Ops:
  6.5 137.9 %copy-start = (bf16[1,1,256,1536]{3,2,1,0:T(8,128)(2,1)S(1)}, bf16[1,1,256,1536]{3,2,1,0:T(8,128)(2,1)}, u32[]{:S(2)}) copy-start(bf16[1,1,256,1536]{3,2,1,0:T(8,128)(2,1)} %param.8) | copy-start | bytes 2359300
  6.5 4.0 %copy-start.1 = (bf16[32,4096]{1,0:T(8,128)(2,1)S(1)}, bf16[32,4096]{1,0:T(8,128)(2,1)}, u32[]{:S(2)}) copy-start(bf16[32,4096]{1,0:T(8,128)(2,1)} %param.5) | copy-start | bytes 786436
  12.4 4.0 %copy-start.3 = (f32[32,8]{0,1:T(8,128)S(1)}, f32[32,8]{0,1:T(8,128)}, u32[]{:S(2)}) copy-start(f32[32,8]{0,1:T(8,128)} %param.7) | copy-start | bytes 3076
  25.7 20.6 %copy-start.2 = (bf16[1,384,256]{2,1,0:T(8,128)(2,1)S(1)}, bf16[1,384,256]{2,1,0:T(8,128)(2,1)}, u32[]{:S(2)}) copy-start(bf16[1,384,256]{2,1,0:T(8,128)(2,1)} %param.9) | copy-start | bytes 589828
  25.7 116.4 %all-to-all-start = ((bf16[128,2,4096]{2,1,0:T(2,128)(2,1)}), bf16[128,2,4096]{2,1,0:T(2,128)(2,1)S(1)}, u32[]{:S(2)}, u32[]{:S(2)}) async-start(bf16[128,2,4096]{2,1,0:T(2,128)(2,1)} %select_convert_fusion), calls=%async_computation | async-start | bytes 4194304 | tf_op jit(solution)/shard_map/all_to_all | solution.py:36
  46.3 153.9 %reduce-scatter.2.cloned.1.call-start = ((), (), s32[]{:S(2)}) async-start(), calls=%async_computation.2 | async-start | bytes 5242880 | tf_op jit(solution)/shard_map/reduce_scatter | solution.py:39
Sparse Core Ops, SparseCore 0:
  149.7 50.4 reduce-scatter.1
where the time goes:
time: 209 us
  waiting for transfers between devices  133 us (64%)
  starting transfers between devices  20.6 us (10%)
  between operations  13.5 us (6%)
  local copies, waits for them, and re-layouts  13.2 us (6%)
  blocking collectives  13.2 us (6%)
  other arithmetic  10.2 us (5%)
  matrix products  5.11 us (2%)
    all_to_all x1, waiting for transfers between devices, shards(): lax.all_to_all(outgoing, 'expert', split_axis=0, concat_axis=0, tiled=True)  82.7 us
    reduce_scatter x1, waiting for transfers between devices, shards(): lax.psum_scatter(lax.dot_general(arrived, reduced, (((0,), (0,)), ((), ()...  50.6 us
    all_to_all x1, starting transfers between devices, shards(): lax.all_to_all(outgoing, 'expert', split_axis=0, concat_axis=0, tiled=True)  20.5 us
    all_gather x1, blocking collectives, shards(): lax.all_gather(projection[0], 'dp', axis=0, tiled=True)  13.2 us
    convert_element_type x1, other arithmetic, shards(): jnp.where(valid[:, None], weight[:, None] * rows, 0.0).astype(jnp.bfloat16)  6.93 us
    dot_general x1, matrix products, shards(): lax.dot_general(arrived, reduced, (((0,), (0,)), ((), ())), preferred_ele...  5.11 us
  transfers between devices with their start and end apart: 2, of which 2 were waited for; matrix products, arithmetic and copies ran while one was open for 0% of the time, Pallas kernels for 0%

commit v1 on v0

--- a/solution.py
+++ b/solution.py
@@ -30,7 +30,9 @@
     hidden = hidden_act[0, 0]
     reduced = jnp.dot(
         hidden,
-        lax.all_gather(projection[0], "dp", axis=0, tiled=True),
+        jnp.concatenate(
+            lax.all_to_all(jnp.stack([projection[0]] * lax.axis_size("dp")), "dp", 0, 0), axis=0
+        ),
         preferred_element_type=jnp.float32,
     ).astype(jnp.bfloat16)
     arrived = lax.all_to_all(outgoing, "expert", split_axis=0, concat_axis=0, tiled=True).reshape(

time: 209 us -> 221 us (1.057)
  blocking collectives: 13.2 us -> 116 us
  waiting for transfers between devices: 133 us -> 58.9 us
  starting transfers between devices: 20.6 us -> 4.23 us
    all_to_all x0 -> x1, blocking collectives: none -> 116 us  [shards(): lax.all_to_all(outgoing, 'expert', split_axis=0, concat_axis=0, tiled=True)]
    all_to_all x1, waiting for transfers between devices: 82.7 us -> 6.45 us  [shards(): lax.all_to_all(jnp.stack([projection[0]] * lax.axis_size('dp')), 'dp', 0, 0)]
    all_to_all x1, starting transfers between devices: 20.5 us -> 4.19 us  [shards(): lax.all_to_all(jnp.stack([projection[0]] * lax.axis_size('dp')), 'dp', 0, 0)]
    all_gather x1 -> x0, blocking collectives: 13.2 us -> none  [shards(): lax.all_gather(projection[0], 'dp', axis=0, tiled=True)]
  transfers between devices with their start and end apart: 2 -> 2, of which waited for: 2 -> 2; matrix products, arithmetic and copies ran while one was open for 0% -> 1% of each run, Pallas kernels for 0% -> 0%
where the time goes in v1:
time: 221 us
  blocking collectives  116 us (52%)
  waiting for transfers between devices  58.9 us (27%)
  local copies, waits for them, and re-layouts  14.2 us (6%)
  between operations  13.5 us (6%)
  other arithmetic  8.82 us (4%)
  matrix products  5.11 us (2%)
  starting transfers between devices  4.23 us (2%)
    all_to_all x1, blocking collectives, shards(): lax.all_to_all(outgoing, 'expert', split_axis=0, concat_axis=0, tiled=True)  116 us
    reduce_scatter x1, waiting for transfers between devices, shards(): lax.psum_scatter(lax.dot_general(arrived, reduced, (((0,), (0,)), ((), ()...  52.4 us
    all_to_all x1, waiting for transfers between devices, shards(): lax.all_to_all(jnp.stack([projection[0]] * lax.axis_size('dp')), 'dp', 0, 0)  6.45 us
    convert_element_type x1, other arithmetic, shards(): jnp.where(valid[:, None], weight[:, None] * rows, 0.0).astype(jnp.bfloat16)  5.6 us
    dot_general x1, matrix products, shards(): lax.dot_general(arrived, reduced, (((0,), (0,)), ((), ())), preferred_ele...  5.11 us
  transfers between devices with their start and end apart: 2, of which 2 were waited for; matrix products, arithmetic and copies ran while one was open for 1% of the time, Pallas kernels for 0%

profile of v1, /device:TPU:1, one launch (start us, length us, event | category | flops | bytes accessed | tf_op | source)
XLA Modules:
  0.0 221.0 jit_solution(14695325288895301090)
XLA Ops:
  6.5 0.0 copy-start
  6.5 0.0 copy-start.1
  6.5 0.8 copy.7
  7.4 0.1 eq.29
  7.5 0.1 eq.25
  7.6 0.7 broadcast_multiply_fusion
  8.3 0.1 copy.9
  8.4 0.2 fusion.3
  8.7 0.1 copy.6
  8.8 0.1 mul.32
  8.8 0.2 fusion.5
  9.1 1.4 scatter_custom_fusion
  10.5 0.0 copy-done.1
  10.5 1.8 gather_fusion.1
  12.4 0.0 copy-start.3
  12.4 4.0 %reshape.76 = f32[128,2,4096]{2,1,0:T(2,128)} reshape(bf16[256,4096]{1,0:T(8,128)(2,1)S(1)} %gather_fusion.1) | data formatting | bytes 6291456 | tf_op jit(solution)/shard_map/convert_element_type | solution.py:26
  16.4 0.0 copy-done.3
  16.4 0.1 copy.11
  16.4 0.1 reshape.73
  16.5 1.9 gather_fusion
  18.5 0.1 mul.34
  18.6 0.2 broadcast_in_dim.31
  18.8 5.6 %select_convert_fusion = bf16[128,2,4096]{2,1,0:T(2,128)(2,1)S(1)} fusion(f32[128,2,4096]{2,1,0:T(2,128)} %reshape.76, pred[128,2]{1,0:T(8,128)(4,1)S(1)} %broadcast_in_dim.31, f32[128,2]{1,0:T(8,128)S(1)} %mul.34), kind=kLoop, calls=%fused_computation.3 | loop fusion | flops 3145728 | bytes 6292736 | tf_op jit(solution)/shard_map/convert_element_type | solution.py:28
  24.4 0.0 copy-start.2
  24.4 116.2 %all_to_all.10 = bf16[128,2,4096]{2,1,0:T(2,128)(2,1)S(1)} all-to-all(bf16[128,2,4096]{2,1,0:T(2,128)(2,1)S(1)} %select_convert_fusion), channel_id=1, replica_groups=mesh['dp'=4,'expert'=128] {'expert'}, dimensions={0} | all-to-all | bytes 4194304 | tf_op jit(solution)/shard_map/all_to_all | solution.py:38
  140.6 0.0 copy-done.2
  140.7 0.9 stack.3
  141.6 4.2 %all-to-all-start.1 = ((bf16[4,384,256]{2,1,0:T(8,128)(2,1)}), bf16[4,384,256]{2,1,0:T(8,128)(2,1)}, u32[]{:S(2)}, u32[]{:S(2)}) async-start(bf16[4,384,256]{2,1,0:T(8,128)(2,1)} %stack.3), calls=%async_computation.1 | async-start | bytes 1572864 | tf_op jit(solution)/shard_map/all_to_all | solution.py:34
  145.8 0.0 reduce-scatter.2.cloned.1.call-start
  145.8 2.2 %reshape.74 = bf16[256,4096]{1,0:T(8,128)(2,1)} reshape(bf16[128,2,4096]{2,1,0:T(2,128)(2,1)S(1)} %all_to_all.10) | data formatting | bytes 4194304 | tf_op jit(solution)/shard_map/reshape | solution.py:38
  148.1 6.5 %all-to-all-done.1 = bf16[4,384,256]{2,1,0:T(8,128)(2,1)} async-done(((bf16[4,384,256]{2,1,0:T(8,128)(2,1)}), bf16[4,384,256]{2,1,0:T(8,128)(2,1)}, u32[]{:S(2)}, u32[]{:S(2)}) %all-to-all-start.1) | async-done | bytes 786464 | tf_op jit(solution)/shard_map/all_to_all | solution.py:34
  154.5 0.0 copy-done
  154.5 5.1 %fusion = f32[4096,256]{1,0:T(8,128)} fusion(bf16[256,4096]{1,0:T(8,128)(2,1)} %reshape.74, bf16[1536,256]{1,0:T(8,128)(2,1)} %bitcast.7, bf16[1,1,256,1536]{3,2,1,0:T(8,128)(2,1)S(1)} %copy-done), kind=kOutput, calls=%fused_computation.5 | convolution fusion | flops 738263040 | bytes 7864320 | tf_op jit(solution)/shard_map/dot_general | solution.py:42
  159.6 0.0 reduce-scatter.2.cloned.1.call-update
  159.7 52.4 %reduce-scatter.2.cloned.1.call-done = f32[1024,256]{1,0:T(8,128)} async-done(((f32[4096,256]{1,0:T(8,128)}), f32[1024,256]{1,0:T(8,128)}) %reduce-scatter.2.cloned.1.call-update) | async-done | bytes 1048592 | tf_op jit(solution)/shard_map/reduce_scatter | solution.py:41
  212.1 2.1 convert_bitcast_fusion
  (11 shorter events, 0.1 us)
Async XLA Ops:
  6.5 148.0 %copy-start = (bf16[1,1,256,1536]{3,2,1,0:T(8,128)(2,1)S(1)}, bf16[1,1,256,1536]{3,2,1,0:T(8,128)(2,1)}, u32[]{:S(2)}) copy-start(bf16[1,1,256,1536]{3,2,1,0:T(8,128)(2,1)} %param.8) | copy-start | bytes 2359300
  6.5 4.0 %copy-start.1 = (bf16[32,4096]{1,0:T(8,128)(2,1)S(1)}, bf16[32,4096]{1,0:T(8,128)(2,1)}, u32[]{:S(2)}) copy-start(bf16[32,4096]{1,0:T(8,128)(2,1)} %param.5) | copy-start | bytes 786436
  12.4 4.0 %copy-start.3 = (f32[32,8]{0,1:T(8,128)S(1)}, f32[32,8]{0,1:T(8,128)}, u32[]{:S(2)}) copy-start(f32[32,8]{0,1:T(8,128)} %param.7) | copy-start | bytes 3076
  24.4 116.3 %copy-start.2 = (bf16[1,384,256]{2,1,0:T(8,128)(2,1)S(1)}, bf16[1,384,256]{2,1,0:T(8,128)(2,1)}, u32[]{:S(2)}) copy-start(bf16[1,384,256]{2,1,0:T(8,128)(2,1)} %param.9) | copy-start | bytes 589828
  141.6 13.0 %all-to-all-start.1 = ((bf16[4,384,256]{2,1,0:T(8,128)(2,1)}), bf16[4,384,256]{2,1,0:T(8,128)(2,1)}, u32[]{:S(2)}, u32[]{:S(2)}) async-start(bf16[4,384,256]{2,1,0:T(8,128)(2,1)} %stack.3), calls=%async_computation.1 | async-start | bytes 1572864 | tf_op jit(solution)/shard_map/all_to_all | solution.py:34
  145.8 66.3 %reduce-scatter.2.cloned.1.call-start = ((), (), s32[]{:S(2)}) async-start(), calls=%async_computation.3 | async-start | bytes 5242880 | tf_op jit(solution)/shard_map/reduce_scatter | solution.py:41
Sparse Core Ops, SparseCore 0:
  159.8 52.2 reduce-scatter.1
